TPU v7x, 32 devices: a whole 2x2x4 slice. The times are simulated.
32 devices in a mesh: dp: 2 (over core), ctx: 8 (over z, y), tp: 2 (over x).
Axes of the slice: x: 2, y: 2, z: 4, core: 2. Of those that a mesh axis runs over, the one named last changes fastest.
Arguments:
- prompt_states: bfloat16 [2048, 2048], P(('dp', 'ctx')), may hold values from -6 to 6
- continuation_states: bfloat16 [8192, 2048], P(('dp', 'ctx')), may hold values from -6 to 6
- continuation_offset: int32 [16], P(('dp', 'ctx')), may hold values from 0 to 511
- attention_gain: bfloat16 [2048], replicated, may hold values from 0.099609375 to 1.8984375
- query_weight: bfloat16 [2048, 1280], P(('dp', 'ctx'), 'tp'), may hold values from -0.125 to 0.125
- key_weight: bfloat16 [2048, 320], P(('dp', 'ctx')), may hold values from -0.125 to 0.125
- value_weight: bfloat16 [2048, 320], P(('dp', 'ctx')), may hold values from -0.125 to 0.125
- query_gain: bfloat16 [64], replicated, may hold values from 0.099609375 to 1.8984375
- key_gain: bfloat16 [64], replicated, may hold values from 0.099609375 to 1.8984375
- output_weight: bfloat16 [1280, 2048], P('tp', ('dp', 'ctx')), may hold values from -6 to 6
- feedforward_gain: bfloat16 [2048], replicated, may hold values from 0.099609375 to 1.8984375
- gate_weight: bfloat16 [2048, 5120], P(('dp', 'ctx'), 'tp'), may hold values from -0.125 to 0.125
- up_weight: bfloat16 [2048, 5120], P(('dp', 'ctx'), 'tp'), may hold values from -0.125 to 0.125
- down_weight: bfloat16 [5120, 2048], P('tp', ('dp', 'ctx')), may hold values from -0.078125 to 0.078125
- grad_prompt: bfloat16 [2048, 2048], P(('dp', 'ctx')), may hold values from -6 to 6
- grad_continuation: bfloat16 [8192, 2048], P(('dp', 'ctx')), may hold values from -6 to 6
Outputs:
- prompt_output: bfloat16 [2048, 2048], P(('dp', 'ctx'))
- continuation_output: bfloat16 [8192, 2048], P(('dp', 'ctx'))
- prompt_input_grad: bfloat16 [2048, 2048], P(('dp', 'ctx'))
- continuation_input_grad: bfloat16 [8192, 2048], P(('dp', 'ctx'))
- attention_gain_grad: float32 [2048], replicated
- query_weight_grad: float32 [2048, 1280], P(('dp', 'ctx'), 'tp')
- key_weight_grad: float32 [2048, 320], P(('dp', 'ctx'))
- value_weight_grad: float32 [2048, 320], P(('dp', 'ctx'))
- query_gain_grad: float32 [64], replicated
- key_gain_grad: float32 [64], replicated
- output_weight_grad: float32 [1280, 2048], P('tp', ('dp', 'ctx'))
- feedforward_gain_grad: float32 [2048], replicated
- gate_weight_grad: float32 [2048, 5120], P(('dp', 'ctx'), 'tp')
- up_weight_grad: float32 [2048, 5120], P(('dp', 'ctx'), 'tp')
- down_weight_grad: float32 [5120, 2048], P('tp', ('dp', 'ctx'))
All inputs are finite; a program needn't handle non-finite values.
Results may differ from a plain program's by a relative error of at most 0.019.
Values may be sent and summed in bfloat16 or wider, within the bound.
No kernel may reach another device: no remote copies, remote signals or barrier semaphores. Data moves between devices by JAX's collectives and lax.ppermute only.
A program may use at most 256 MiB of HBM per device.

v0:
```python
from functools import partial
import jax
import jax.numpy as jnp
from jax import lax
from jax.sharding import PartitionSpec as P

epsilon = 1e-06


def rms_norm(values, norm_gain):
    scale = lax.rsqrt(jnp.mean(values * values, axis=-1, keepdims=True) + epsilon)
    return values * scale * norm_gain


def rope_tables(positions, width):
    half_width = width // 2
    freqs = 10000.0 ** (-(2.0 * jnp.arange(half_width, dtype=jnp.float32)) / width)
    angles = positions[:, None] * freqs[None, :]
    angles = jnp.concatenate([angles, angles], axis=1)
    return (jnp.cos(angles), jnp.sin(angles))


def head_prep(raw_heads, norm_gain, cosine_table, sine_table):
    normed = rms_norm(raw_heads, norm_gain)
    half_width = raw_heads.shape[-1] // 2
    turned = jnp.concatenate([-normed[..., half_width:], normed[..., :half_width]], axis=-1)
    return normed * cosine_table[:, None, :] + turned * sine_table[:, None, :]


def swiglu(gate_rows, up_rows):
    return jax.nn.silu(gate_rows) * up_rows


def contract_last(left_rows, right_rows):
    return lax.dot_general(
        left_rows, right_rows, (((1,), (1,)), ((), ())), preferred_element_type=jnp.float32
    )


def contract_first(left_rows, right_rows):
    return lax.dot_general(
        left_rows, right_rows, (((0,), (0,)), ((), ())), preferred_element_type=jnp.float32
    )


def fold_columns(inputs, pieces):
    return tuple(
        (
            jnp.dot(inputs, weight_piece, preferred_element_type=jnp.float32)
            for weight_piece in pieces
        )
    )


def tensor_sum(values):
    return lax.psum(values.astype(jnp.bfloat16), "tp").astype(jnp.float32)


def on_device(
    prompt_states,
    continuation_states,
    continuation_offset,
    attention_gain,
    query_weight,
    key_weight,
    value_weight,
    query_gain,
    key_gain,
    output_weight,
    feedforward_gain,
    gate_weight,
    up_weight,
    down_weight,
    grad_prompt,
    grad_continuation,
):
    prompt_here = prompt_states.shape[0]
    cont_length = continuation_states.shape[0]
    rows_here = prompt_here + cont_length
    prompt_length = prompt_here * lax.axis_size("ctx")
    key_count = prompt_length + cont_length
    head_size = query_gain.shape[0]
    local_heads = query_weight.shape[1] // head_size
    shared_heads = key_weight.shape[1] // head_size
    group_size = local_heads * lax.axis_size("tp") // shared_heads
    context_rank = lax.axis_index("ctx")
    tensor_rank = lax.axis_index("tp")
    inputs = jnp.concatenate([prompt_states, continuation_states], axis=0)
    input_float = inputs.astype(jnp.float32)
    row_ids = jnp.arange(rows_here, dtype=jnp.int32)
    prompt_place = context_rank * prompt_here + row_ids
    positions = jnp.where(
        row_ids < prompt_here,
        prompt_place,
        prompt_length + continuation_offset[0] + row_ids - prompt_here,
    ).astype(jnp.float32)
    cosine_table, sine_table = rope_tables(positions, head_size)
    key_ids = jnp.arange(key_count, dtype=jnp.int32)
    allowed = jnp.where(
        (row_ids < prompt_here)[:, None],
        key_ids[None, :] <= prompt_place[:, None],
        (key_ids[None, :] < prompt_length)
        | (key_ids[None, :] - prompt_length <= (row_ids - prompt_here)[:, None]),
    )
    rotate = partial(head_prep, cosine_table=cosine_table, sine_table=sine_table)
    normed, attn_norm_back = jax.vjp(rms_norm, input_float, attention_gain.astype(jnp.float32))
    normed_low = normed.astype(jnp.bfloat16)
    query_raw, key_raw, value_raw = fold_columns(
        normed_low,
        (
            lax.all_gather(query_weight, ("dp", "ctx"), axis=0, tiled=True),
            lax.all_gather(key_weight, ("dp", "ctx"), axis=0, tiled=True),
            lax.all_gather(value_weight, ("dp", "ctx"), axis=0, tiled=True),
        ),
    )
    query_rot, query_back = jax.vjp(
        rotate, query_raw.reshape(rows_here, local_heads, head_size), query_gain.astype(jnp.float32)
    )
    query_low = query_rot.reshape(rows_here, local_heads * head_size).astype(jnp.bfloat16)
    key_rot, key_back = jax.vjp(
        rotate, key_raw.reshape(rows_here, shared_heads, head_size), key_gain.astype(jnp.float32)
    )
    key_low = key_rot.reshape(rows_here, shared_heads * head_size).astype(jnp.bfloat16)
    value_low = value_raw.astype(jnp.bfloat16)
    prompt_keys, prompt_values = (
        lax.all_gather(key_low[:prompt_here], "ctx", axis=0, tiled=True),
        lax.all_gather(value_low[:prompt_here], "ctx", axis=0, tiled=True),
    )
    all_keys = jnp.concatenate([prompt_keys, key_low[prompt_here:]], axis=0)
    all_values = jnp.concatenate([prompt_values, value_low[prompt_here:]], axis=0)

    def head_slices(head_index):
        shared_index = (tensor_rank * local_heads + head_index) // group_size
        query_head = lax.dynamic_slice_in_dim(query_low, head_index * head_size, head_size, 1)
        key_head = lax.dynamic_slice_in_dim(all_keys, shared_index * head_size, head_size, 1)
        value_head = lax.dynamic_slice_in_dim(all_values, shared_index * head_size, head_size, 1)
        return (query_head, key_head, value_head, shared_index)

    def scores_of(query_head, key_head):
        scores = contract_last(query_head, key_head) * 0.125
        return jnp.where(allowed, scores, -1e30)

    def head_forward(head_index):
        query_head, key_head, value_head, shared_index = head_slices(head_index)
        scores = scores_of(query_head, key_head)
        row_max = jnp.max(scores, axis=1, keepdims=True)
        weights = jnp.exp(scores - row_max)
        totals = jnp.sum(weights, axis=1, keepdims=True)
        probabilities = (weights / totals).astype(jnp.bfloat16)
        combined = jnp.dot(probabilities, value_head, preferred_element_type=jnp.float32)
        return (combined, (row_max + jnp.log(totals))[:, 0])

    per_head, log_sums = lax.map(head_forward, jnp.arange(local_heads, dtype=jnp.int32))
    attended_low = (
        jnp.transpose(per_head, (1, 0, 2))
        .reshape(rows_here, local_heads * head_size)
        .astype(jnp.bfloat16)
    )
    output_full, down_full = (
        lax.all_gather(output_weight, ("dp", "ctx"), axis=1, tiled=True),
        lax.all_gather(down_weight, ("dp", "ctx"), axis=1, tiled=True),
    )
    resid = input_float + tensor_sum(
        jnp.dot(attended_low, output_full, preferred_element_type=jnp.float32)
    )
    normed_two, ffn_norm_back = jax.vjp(rms_norm, resid, feedforward_gain.astype(jnp.float32))
    normed_two_low = normed_two.astype(jnp.bfloat16)
    gate_rows, up_rows = fold_columns(
        normed_two_low,
        (
            lax.all_gather(gate_weight, ("dp", "ctx"), axis=0, tiled=True),
            lax.all_gather(up_weight, ("dp", "ctx"), axis=0, tiled=True),
        ),
    )
    hidden, swiglu_back = jax.vjp(swiglu, gate_rows, up_rows)
    hidden_low = hidden.astype(jnp.bfloat16)
    output = resid + tensor_sum(jnp.dot(hidden_low, down_full, preferred_element_type=jnp.float32))
    prompt_output = output[:prompt_here].astype(jnp.bfloat16)
    continuation_output = output[prompt_here:].astype(jnp.bfloat16)
    grad_out = jnp.concatenate([grad_prompt, grad_continuation], axis=0)
    grad_down = contract_first(hidden_low, grad_out)
    output_back, down_back = (
        lax.all_gather(output_weight, ("dp", "ctx"), axis=1, tiled=True),
        lax.all_gather(down_weight, ("dp", "ctx"), axis=1, tiled=True),
    )
    grad_hidden = contract_last(grad_out, down_back)
    grad_gate, grad_up = swiglu_back(grad_hidden)
    grad_gate_low = grad_gate.astype(jnp.bfloat16)
    grad_up_low = grad_up.astype(jnp.bfloat16)
    grad_gate_weight = contract_first(normed_two_low, grad_gate_low)
    grad_up_weight = contract_first(normed_two_low, grad_up_low)
    pieces = (
        lax.all_gather(gate_weight, ("dp", "ctx"), axis=0, tiled=True),
        lax.all_gather(up_weight, ("dp", "ctx"), axis=0, tiled=True),
    )
    product = contract_last(grad_gate_low, pieces[0]) + contract_last(grad_up_low, pieces[1])
    grad_resid_part, grad_ffn_gain = ffn_norm_back(tensor_sum(product))
    grad_resid = grad_out.astype(jnp.float32) + grad_resid_part
    grad_resid_low = grad_resid.astype(jnp.bfloat16)
    grad_output_weight = contract_first(attended_low, grad_resid_low)
    grad_attended = contract_last(grad_resid_low, output_back).astype(jnp.bfloat16)

    def head_backward(carry, head_index):
        key_totals, value_totals = carry
        query_head, key_head, value_head, shared_index = head_slices(head_index)
        grad_head = lax.dynamic_slice_in_dim(grad_attended, head_index * head_size, head_size, 1)
        probabilities = jnp.exp(scores_of(query_head, key_head) - log_sums[head_index][:, None])
        grad_value = contract_first(probabilities.astype(jnp.bfloat16), grad_head)
        grad_probs = contract_last(grad_head, value_head)
        delta = jnp.sum(probabilities * grad_probs, axis=1, keepdims=True)
        grad_scores = (probabilities * (grad_probs - delta) * 0.125).astype(jnp.bfloat16)
        grad_query = jnp.dot(grad_scores, key_head, preferred_element_type=jnp.float32)
        grad_key = contract_first(grad_scores, query_head)
        column = shared_index * head_size
        key_totals = lax.dynamic_update_slice_in_dim(
            key_totals,
            lax.dynamic_slice_in_dim(key_totals, column, head_size, 1) + grad_key,
            column,
            1,
        )
        value_totals = lax.dynamic_update_slice_in_dim(
            value_totals,
            lax.dynamic_slice_in_dim(value_totals, column, head_size, 1) + grad_value,
            column,
            1,
        )
        return ((key_totals, value_totals), grad_query)

    zeros_keys = jnp.zeros((key_count, shared_heads * head_size), jnp.float32)
    (grad_keys, grad_values), grad_queries = lax.scan(
        head_backward, (zeros_keys, zeros_keys), jnp.arange(local_heads, dtype=jnp.int32)
    )
    grad_query_rot = jnp.transpose(grad_queries, (1, 0, 2))
    grad_query_raw, grad_query_gain = query_back(grad_query_rot)
    grad_query_low = grad_query_raw.reshape(rows_here, local_heads * head_size).astype(jnp.bfloat16)
    prompt_key_grad, prompt_value_grad = (
        lax.psum_scatter(
            grad_keys[:prompt_length].astype(jnp.bfloat16), "ctx", scatter_dimension=0, tiled=True
        ).astype(jnp.float32),
        lax.psum_scatter(
            grad_values[:prompt_length].astype(jnp.bfloat16), "ctx", scatter_dimension=0, tiled=True
        ).astype(jnp.float32),
    )
    own_key_grad = jnp.concatenate([prompt_key_grad, grad_keys[prompt_length:]], axis=0)
    own_value_grad = jnp.concatenate([prompt_value_grad, grad_values[prompt_length:]], axis=0)
    own_key_grad, own_value_grad, grad_query_gain = (
        lax.psum(own_key_grad.astype(jnp.bfloat16), "tp").astype(jnp.float32),
        lax.psum(own_value_grad.astype(jnp.bfloat16), "tp").astype(jnp.float32),
        lax.psum(grad_query_gain.astype(jnp.bfloat16), "tp").astype(jnp.float32),
    )
    grad_key_raw, grad_key_gain = key_back(own_key_grad.reshape(rows_here, shared_heads, head_size))
    grad_key_low = grad_key_raw.reshape(rows_here, shared_heads * head_size).astype(jnp.bfloat16)
    grad_value_low = own_value_grad.astype(jnp.bfloat16)
    grad_query_weight = contract_first(normed_low, grad_query_low)
    grad_key_weight = contract_first(normed_low, grad_key_low)
    grad_value_weight = contract_first(normed_low, grad_value_low)
    pieces = (
        lax.all_gather(query_weight, ("dp", "ctx"), axis=0, tiled=True),
        lax.all_gather(key_weight, ("dp", "ctx"), axis=0, tiled=True),
        lax.all_gather(value_weight, ("dp", "ctx"), axis=0, tiled=True),
    )
    query_part = contract_last(grad_query_low, pieces[0])
    shared_part = contract_last(grad_key_low, pieces[1]) + contract_last(grad_value_low, pieces[2])
    grad_normed = tensor_sum(query_part) + shared_part
    grad_input_part, grad_attn_gain = attn_norm_back(grad_normed)
    grad_input = (grad_resid + grad_input_part).astype(jnp.bfloat16)
    query_done, key_done, value_done, gate_done, up_done = (
        lax.psum_scatter(grad_query_weight, ("dp", "ctx"), scatter_dimension=0, tiled=True),
        lax.psum_scatter(grad_key_weight, ("dp", "ctx"), scatter_dimension=0, tiled=True),
        lax.psum_scatter(grad_value_weight, ("dp", "ctx"), scatter_dimension=0, tiled=True),
        lax.psum_scatter(grad_gate_weight, ("dp", "ctx"), scatter_dimension=0, tiled=True),
        lax.psum_scatter(grad_up_weight, ("dp", "ctx"), scatter_dimension=0, tiled=True),
    )
    outward = (
        lax.psum_scatter(grad_output_weight, ("dp", "ctx"), scatter_dimension=1, tiled=True),
        lax.psum_scatter(grad_down, ("dp", "ctx"), scatter_dimension=1, tiled=True),
    )
    gain_sums = lax.psum(
        (grad_attn_gain, grad_ffn_gain, grad_query_gain, grad_key_gain), ("dp", "ctx")
    )
    return (
        prompt_output,
        continuation_output,
        grad_input[:prompt_here],
        grad_input[prompt_here:],
        gain_sums[0],
        query_done,
        key_done,
        value_done,
        gain_sums[2],
        gain_sums[3],
        outward[0],
        gain_sums[1],
        gate_done,
        up_done,
        outward[1],
    )


def solution(mesh):
    in_specs = (
        P(("dp", "ctx"), None),
        P(("dp", "ctx"), None),
        P(("dp", "ctx")),
        P(),
        P(("dp", "ctx"), "tp"),
        P(("dp", "ctx"), None),
        P(("dp", "ctx"), None),
        P(),
        P(),
        P("tp", ("dp", "ctx")),
        P(),
        P(("dp", "ctx"), "tp"),
        P(("dp", "ctx"), "tp"),
        P("tp", ("dp", "ctx")),
        P(("dp", "ctx"), None),
        P(("dp", "ctx"), None),
    )
    out_specs = (
        P(("dp", "ctx"), None),
        P(("dp", "ctx"), None),
        P(("dp", "ctx"), None),
        P(("dp", "ctx"), None),
        P(),
        P(("dp", "ctx"), "tp"),
        P(("dp", "ctx"), None),
        P(("dp", "ctx"), None),
        P(),
        P(),
        P("tp", ("dp", "ctx")),
        P(),
        P(("dp", "ctx"), "tp"),
        P(("dp", "ctx"), "tp"),
        P("tp", ("dp", "ctx")),
    )
    return jax.shard_map(
        on_device, mesh=mesh, in_specs=in_specs, out_specs=out_specs, check_vma=False
    )
```

profile of v0, /device:TPU:0, one launch (start us, length us, event | category | flops | bytes accessed | tf_op | source)
XLA Modules:
  0.0 2214.9 jit_solution(14134863726572111871)
XLA Ops:
  17.5 33.2 %all-gather.10.cloned.1.call-done = bf16[2048,320]{0,1:T(8,128)(2,1)} async-done(((bf16[128,320]{0,1:T(8,128)(2,1)}), bf16[2048,320]{0,1:T(8,128)(2,1)}) %all-gather.10.cloned.1.call-update) | async-done | bytes 1310736 | tf_op jit(solution)/shard_map/all_gather | solution.py:112
  55.9 34.0 %all-gather.12.cloned.1.call-done = bf16[2048,320]{0,1:T(8,128)(2,1)} async-done(((bf16[128,320]{0,1:T(8,128)(2,1)}), bf16[2048,320]{0,1:T(8,128)(2,1)}) %all-gather.12.cloned.1.call-update) | async-done | bytes 1310736 | tf_op jit(solution)/shard_map/all_gather | solution.py:113
  94.0 30.2 %all_gather.36 = bf16[1024,320]{0,1:T(8,128)(2,1)S(1)} all-gather(bf16[128,320]{0,1:T(8,128)(2,1)S(1)} %slice.74), channel_id=1, replica_groups=mesh['dp'=2,'ctx'=8,'tp'=2] {'ctx'}, dimensions={0}, use_global_device_ids=true | all-gather | bytes 737280 | tf_op jit(solution)/shard_map/all_gather | solution.py:126
  127.5 29.9 %all_gather.38 = bf16[1024,320]{0,1:T(8,128)(2,1)S(1)} all-gather(bf16[128,320]{0,1:T(8,128)(2,1)S(1)} %slice.76), channel_id=1, replica_groups=mesh['dp'=2,'ctx'=8,'tp'=2] {'ctx'}, dimensions={0}, use_global_device_ids=true | all-gather | bytes 737280 | tf_op jit(solution)/shard_map/all_gather | solution.py:127
  169.9 124.1 %while.34 = (s32[]{:T(128)}, bf16[10,640,64]{1,2,0:T(8,128)(2,1)}, f32[10,640]{1,0:T(8,128)}, s32[10]{0:T(128)S(1)}, bf16[640,640]{1,0:T(8,128)(2,1)S(1)}, /*ind...) while((s32[]{:T(128)}, bf16[10,640,64]{1,2,0:T(8,128)(2,1)}, ...), condition=%wide.region_6.7_spmd.clone.clone, body=%wide.region_3.6_spmd.clone.sunk.clone | while | flops 263454112 | bytes 28690356 | solution.py:153
  307.4 65.5 %all-reduce.10.cloned.1.call-done = bf16[640,2048]{1,0:T(8,128)(2,1)} async-done(((bf16[640,2048]{1,0:T(8,128)(2,1)}), bf16[640,2048]{1,0:T(8,128)(2,1)}) %all-reduce.10.cloned.1.call-update) | async-done | bytes 2621456 | tf_op jit(solution)/shard_map/psum | solution.py:56
  378.7 84.5 %all-gather.16.cloned.1.call-done = bf16[2048,2560]{1,0:T(8,128)(2,1)} async-done(((bf16[128,2560]{1,0:T(8,128)(2,1)}), bf16[2048,2560]{1,0:T(8,128)(2,1)}) %all-gather.16.cloned.1.call-update) | async-done | bytes 10485776 | tf_op jit(solution)/shard_map/all_gather | solution.py:171
  475.4 76.2 %all-gather.18.cloned.1.call-done = bf16[2048,2560]{1,0:T(8,128)(2,1)} async-done(((bf16[128,2560]{1,0:T(8,128)(2,1)}), bf16[2048,2560]{1,0:T(8,128)(2,1)}) %all-gather.18.cloned.1.call-update) | async-done | bytes 10485776 | tf_op jit(solution)/shard_map/all_gather | solution.py:172
  563.8 79.1 %all-gather.20.cloned.1.call-done = bf16[2560,2048]{1,0:T(8,128)(2,1)} async-done(((bf16[2560,128]{1,0:T(8,128)(2,1)}), bf16[2560,2048]{1,0:T(8,128)(2,1)}) %all-gather.20.cloned.1.call-update) | async-done | bytes 10485776 | tf_op jit(solution)/shard_map/all_gather | solution.py:161
  642.9 17.8 multiply_convert_fusion.1
  682.7 72.6 %all-reduce.12.cloned.1.call-done = bf16[640,2048]{1,0:T(8,128)(2,1)} async-done(((bf16[640,2048]{1,0:T(8,128)(2,1)}), bf16[640,2048]{1,0:T(8,128)(2,1)}) %all-reduce.12.cloned.1.call-update) | async-done | bytes 2621456 | tf_op jit(solution)/shard_map/psum | solution.py:56
  769.4 208.5 %while.35 = (s32[]{:T(128)}, f32[1536,320]{0,1:T(8,128)}, f32[1536,320]{0,1:T(8,128)}, f32[10,640,64]{1,2,0:T(8,128)}, s32[10]{0:T(128)S(1)}, /*index=5*/s32[]{:...) while((s32[]{:T(128)}, f32[1536,320]{0,1:T(8,128)}, ...), condition=%wide.region_14.15_spmd.clone.clone, body=%wide.region_12.14_spmd.clone.sunk.clone | while | flops 643104128 | bytes 48826372 | solution.py:230
  1008.4 36.1 %reduce-scatter.30.cloned.1.call-done = bf16[128,320]{1,0:T(8,128)(2,1)} async-done(((bf16[1024,320]{1,0:T(8,128)(2,1)}), bf16[128,320]{1,0:T(8,128)(2,1)}) %reduce-scatter.30.cloned.1.call-update) | async-done | bytes 81936
  1046.2 63.9 %reduce-scatter.28.cloned.1.call-done = bf16[128,320]{1,0:T(8,128)(2,1)} async-done(((bf16[1024,320]{1,0:T(8,128)(2,1)}), bf16[128,320]{1,0:T(8,128)(2,1)}) %reduce-scatter.28.cloned.1.call-update) | async-done | bytes 81936
  1129.4 132.1 %all-reduce.14.cloned.1.call-done = (bf16[640,2048]{1,0:T(8,128)(2,1)}, bf16[640,5,64]{0,2,1:T(8,128)(2,1)}, bf16[640,2048]{1,0:T(8,128)(2,1)}, bf16[640,320]{0,1:T(8,128)(2,1)}) async-done(((bf16[640,2048]{1,0:T(8,128)(2,1)}, bf16[640,5,64]{0,2,1:T(8,128)(2,1)}, bf16[640,2048]{1,0:T(8,128)(2,1)}, bf16[640,320]{0,1:T(8,128)(2,1)}), (bf16[640,2048]{1,0:T(8,128)(2,1)}, bf16[640,5,64]{0,2,1:T(8,128)(2,1)}, ...) | async-done | bytes 6062096 | tf_op jit(solution)/shard_map/psum | solution.py:56
  1272.8 15.2 fusion.80
  1288.1 14.9 fusion.81
  1341.1 61.1 %all-reduce.4 = (f32[2048]{0:T(1024)}, f32[64]{0:T(128)}, f32[64]{0:T(128)}, f32[2048]{0:T(1024)}) all-reduce(f32[2048]{0:T(1024)S(1)} %get-tuple-element.423, bf16[64]{0:T(256)(128)(2,1)S(1)} %psum.84, f32[64]{0:T(128)S(1)} %get-tuple-element.427, f32[2048]{0:T(1024)S(1)} %copy-done.46), channel_id=1, replica_groups=mesh['dp'=2,'ctx'=8,'tp'=2] {'dp','ctx'}, use_global_device_ids=true, to_apply=%region_24.25 | all-reduce | flops 4224 | bytes 33664 | tf_op jit(solution)/shard_map/psum | solution.py:278
  1402.2 25.7 %reduce-scatter.14.cloned.1.call-done = f32[128,640]{1,0:T(8,128)} async-done(((f32[2048,640]{1,0:T(8,128)}), f32[128,640]{1,0:T(8,128)}) %reduce-scatter.14.cloned.1.call-update) | async-done | bytes 327696 | tf_op jit(solution)/shard_map/reduce_scatter | solution.py:268
  1427.9 67.5 %reduce-scatter.16.cloned.1.call-done = f32[128,320]{0,1:T(8,128)} async-done(((f32[2048,320]{0,1:T(8,128)}), f32[128,320]{0,1:T(8,128)}) %reduce-scatter.16.cloned.1.call-update) | async-done | bytes 163856 | tf_op jit(solution)/shard_map/reduce_scatter | solution.py:269
  1495.4 67.6 %reduce-scatter.18.cloned.1.call-done = f32[128,320]{0,1:T(8,128)} async-done(((f32[2048,320]{0,1:T(8,128)}), f32[128,320]{0,1:T(8,128)}) %reduce-scatter.18.cloned.1.call-update) | async-done | bytes 163856 | tf_op jit(solution)/shard_map/reduce_scatter | solution.py:270
  1563.0 215.0 %reduce-scatter.22.cloned.1.call-done = f32[128,2560]{1,0:T(8,128)} async-done(((f32[2048,2560]{1,0:T(8,128)}), f32[128,2560]{1,0:T(8,128)}) %reduce-scatter.22.cloned.1.call-update) | async-done | bytes 1310736 | tf_op jit(solution)/shard_map/reduce_scatter | solution.py:271
  1778.0 215.1 %reduce-scatter.24.cloned.1.call-done = f32[128,2560]{1,0:T(8,128)} async-done(((f32[2048,2560]{1,0:T(8,128)}), f32[128,2560]{1,0:T(8,128)}) %reduce-scatter.24.cloned.1.call-update) | async-done | bytes 1310736 | tf_op jit(solution)/shard_map/reduce_scatter | solution.py:272
  1993.1 215.1 %reduce-scatter.26.cloned.1.call-done = f32[2560,128]{1,0:T(8,128)} async-done(((f32[2560,2048]{1,0:T(8,128)}), f32[2560,128]{1,0:T(8,128)}) %reduce-scatter.26.cloned.1.call-update) | async-done | bytes 1310736 | tf_op jit(solution)/shard_map/reduce_scatter | solution.py:276
  (450 shorter events, 500.2 us)
Async XLA Ops:
  7.2 43.4 %all-gather.10.cloned.1.call-start = ((), (), s32[]{:S(2)}) async-start(), calls=%async_computation.10 | async-start | bytes 1392640 | tf_op jit(solution)/shard_map/all_gather | solution.py:112
  8.0 81.9 %all-gather.12.cloned.1.call-start = ((), (), s32[]{:S(2)}) async-start(), calls=%async_computation.11 | async-start | bytes 1392640 | tf_op jit(solution)/shard_map/all_gather | solution.py:113
  8.7 152.1 %all-gather.8.cloned.1.call-start = ((), (), s32[]{:S(2)}) async-start(), calls=%async_computation.9 | async-start | bytes 2785280 | tf_op jit(solution)/shard_map/all_gather | solution.py:111
  9.5 284.6 %all-gather.14.cloned.1.call-start = ((), (), s32[]{:S(2)}) async-start(), calls=%async_computation.12 | async-start | bytes 2785280 | tf_op jit(solution)/shard_map/all_gather | solution.py:160
  10.0 362.9 %all-reduce.10.cloned.1.call-start = ((), (), s32[]{:S(2)}) async-start(), calls=%async_computation.13 | async-start | bytes 5242880 | tf_op jit(solution)/shard_map/psum | solution.py:56
  15.1 151.6 %copy-start.20 = (f32[640,64]{0,1:T(8,128)}, f32[640,64]{0,1:T(8,128)S(1)}, u32[]{:S(2)}) copy-start(f32[640,64]{0,1:T(8,128)S(1)} %get-tuple-element.514) | copy-start | bytes 491524
  15.1 151.7 %copy-start.15 = (f32[640,64]{0,1:T(8,128)}, f32[640,64]{0,1:T(8,128)S(1)}, u32[]{:S(2)}) copy-start(f32[640,64]{0,1:T(8,128)S(1)} %get-tuple-element.513) | copy-start | bytes 491524
  15.2 150.6 %copy-start.49 = (f32[64]{0:T(128)}, f32[64]{0:T(128)S(1)}, u32[]{:S(2)}) copy-start(f32[64]{0:T(128)S(1)} %convert_element_type.141) | copy-start | bytes 772
  299.8 163.3 %all-gather.16.cloned.1.call-start = ((), (), s32[]{:S(2)}) async-start(), calls=%async_computation.14 | async-start | bytes 11141120 | tf_op jit(solution)/shard_map/all_gather | solution.py:171
  300.4 251.3 %all-gather.18.cloned.1.call-start = ((), (), s32[]{:S(2)}) async-start(), calls=%async_computation.15 | async-start | bytes 11141120 | tf_op jit(solution)/shard_map/all_gather | solution.py:172
  301.2 341.8 %all-gather.20.cloned.1.call-start = ((), (), s32[]{:S(2)}) async-start(), calls=%async_computation.16 | async-start | bytes 11141120 | tf_op jit(solution)/shard_map/all_gather | solution.py:161
  301.9 453.4 %all-reduce.12.cloned.1.call-start = ((), (), s32[]{:S(2)}) async-start(), calls=%async_computation.17 | async-start | bytes 5242880 | tf_op jit(solution)/shard_map/psum | solution.py:56
  682.6 361.8 %reduce-scatter.30.cloned.1.call-start = ((), (), s32[]{:S(2)}) async-start(), calls=%async_computation.26 | async-start | bytes 884736
  981.8 128.4 %reduce-scatter.28.cloned.1.call-start = ((), (), s32[]{:S(2)}) async-start(), calls=%async_computation.25 | async-start | bytes 884736
  999.2 262.3 %all-reduce.14.cloned.1.call-start = ((), (), s32[]{:S(2)}) async-start(), calls=%async_computation.27 | async-start | bytes 12124160 | tf_op jit(solution)/shard_map/psum | solution.py:56
  1112.0 290.2 %reduce-scatter.20.cloned.1.call-start = ((), (), s32[]{:S(2)}) async-start(), calls=%async_computation.21 | async-start | bytes 5570560 | tf_op jit(solution)/shard_map/reduce_scatter | solution.py:275
  1121.4 306.5 %reduce-scatter.14.cloned.1.call-start = ((), (), s32[]{:S(2)}) async-start(), calls=%async_computation.18 | async-start | bytes 5570560 | tf_op jit(solution)/shard_map/reduce_scatter | solution.py:268
  1129.2 133.6 %copy-start.10 = (f32[640,320]{0,1:T(8,128)S(1)}, f32[640,320]{0,1:T(8,128)}, u32[]{:S(2)}) copy-start(f32[640,320]{0,1:T(8,128)} %copy-done.9) | copy-start | bytes 2457604
  1129.2 133.6 %copy-start.35 = (f32[640,5]{0,1:T(8,128)S(1)}, f32[640,5]{0,1:T(8,128)}, u32[]{:S(2)}) copy-start(f32[640,5]{0,1:T(8,128)} %copy-done.34) | copy-start | bytes 38404
  1129.2 366.2 %reduce-scatter.16.cloned.1.call-start = ((), (), s32[]{:S(2)}) async-start(), calls=%async_computation.19 | async-start | bytes 2785280 | tf_op jit(solution)/shard_map/reduce_scatter | solution.py:269
  1267.3 295.7 %reduce-scatter.18.cloned.1.call-start = ((), (), s32[]{:S(2)}) async-start(), calls=%async_computation.20 | async-start | bytes 2785280 | tf_op jit(solution)/shard_map/reduce_scatter | solution.py:270
  1272.8 505.2 %reduce-scatter.22.cloned.1.call-start = ((), (), s32[]{:S(2)}) async-start(), calls=%async_computation.22 | async-start | bytes 22282240 | tf_op jit(solution)/shard_map/reduce_scatter | solution.py:271
  1288.0 705.0 %reduce-scatter.24.cloned.1.call-start = ((), (), s32[]{:S(2)}) async-start(), calls=%async_computation.23 | async-start | bytes 22282240 | tf_op jit(solution)/shard_map/reduce_scatter | solution.py:272
  1303.0 905.1 %reduce-scatter.26.cloned.1.call-start = ((), (), s32[]{:S(2)}) async-start(), calls=%async_computation.24 | async-start | bytes 22282240 | tf_op jit(solution)/shard_map/reduce_scatter | solution.py:276
  (75 other events, 642.4 us)
Sparse Core Ops, SparseCore 0:
  10.1 40.4 all-gather.9
  52.7 37.0 all-gather.11
  92.1 45.4 all-gather.7
  139.5 45.6 all-gather.13
  300.0 72.8 all-reduce.9
  375.2 87.8 all-gather.15
  465.6 86.0 all-gather.17
  554.0 88.9 all-gather.19
  682.7 72.5 all-reduce.11
  981.9 62.4 reduce-scatter.29
  1048.7 61.4 reduce-scatter.27
  1113.2 148.2 all-reduce.13
  1266.5 78.7 reduce-scatter.19
  1350.1 77.7 reduce-scatter.13
  1432.6 62.8 reduce-scatter.15
  1500.1 62.8 reduce-scatter.17
  1568.1 209.8 reduce-scatter.21
  1783.1 209.9 reduce-scatter.23
  1998.3 209.7 reduce-scatter.25
where the time goes:
time: 2220 us; the launch traced here: 2210 us
  waiting for transfers between devices  1490 us (67%)
  matrix products  399 us (18%)
  blocking collectives  126 us (6%)
  local copies, waits for them, and re-layouts  86.6 us (4%)
  other arithmetic  51.4 us (2%)
  loops' own time  46.6 us (2%)
    psum x3, waiting for transfers between devices, tensor_sum(): return lax.psum(values.astype(jnp.bfloat16), 'tp').astype(jnp.float32)  270 us
    reduce_scatter x1, waiting for transfers between devices, on_device(): lax.psum_scatter(grad_up_weight, ('dp', 'ctx'), scatter_dimension=0, tile...  215 us
    reduce_scatter x1, waiting for transfers between devices, on_device(): lax.psum_scatter(grad_down, ('dp', 'ctx'), scatter_dimension=1, tiled=True)  215 us
    reduce_scatter x1, waiting for transfers between devices, on_device(): lax.psum_scatter(grad_gate_weight, ('dp', 'ctx'), scatter_dimension=0, ti...  215 us
    dot_general x37, matrix products, contract_last(): lax.dot_general(left_rows, right_rows, (((1,), (1,)), ((), ())), preferre...  169 us
    dot_general x27, matrix products, contract_first(): lax.dot_general(left_rows, right_rows, (((0,), (0,)), ((), ())), preferre...  114 us
    unnamed x21, waiting for transfers between devices  105 us
    all_gather x1, waiting for transfers between devices, on_device(): lax.all_gather(gate_weight, ('dp', 'ctx'), axis=0, tiled=True)  84.5 us
  transfers between devices with their start and end apart: 19, of which 16 were waited for; matrix products, arithmetic and copies ran while one was open for 12% of the time, Pallas kernels for 0%

commit v1 on v0

--- a/solution.py
+++ b/solution.py
@@ -5,6 +5,22 @@
 from jax.sharding import PartitionSpec as P
 
 epsilon = 1e-06
+
+
+def collect(x, axis, dim):
+    ways, here, lap = (lax.axis_size(axis), lax.axis_index(axis), x.shape[dim])
+    lengths = [n * ways if d == dim else n for d, n in enumerate(x.shape)]
+    full = lax.dynamic_update_slice_in_dim(jnp.zeros(lengths, x.dtype), x, here * lap, axis=dim)
+    going_up = going_down = x
+    for far in range(1, ways // 2 + 1):
+        going_up = lax.ppermute(going_up, axis, [(d, (d + 1) % ways) for d in range(ways)])
+        full = lax.dynamic_update_slice_in_dim(full, going_up, (here - far) % ways * lap, axis=dim)
+        if 2 * far < ways:
+            going_down = lax.ppermute(going_down, axis, [(d, (d - 1) % ways) for d in range(ways)])
+            full = lax.dynamic_update_slice_in_dim(
+                full, going_down, (here + far) % ways * lap, axis=dim
+            )
+    return full
 
 
 def rms_norm(values, norm_gain):
@@ -169,7 +185,7 @@
         normed_two_low,
         (
             lax.all_gather(gate_weight, ("dp", "ctx"), axis=0, tiled=True),
-            lax.all_gather(up_weight, ("dp", "ctx"), axis=0, tiled=True),
+            collect(up_weight, ("dp", "ctx"), 0),
         ),
     )
     hidden, swiglu_back = jax.vjp(swiglu, gate_rows, up_rows)

time: 2220 us -> 2280 us (1.027)
  starting transfers between devices: 1.15 us -> 71.7 us
  waiting for transfers between devices: 1490 us -> 1450 us
  local copies, waits for them, and re-layouts: 86.6 us -> 110 us
    ppermute x0 -> x15, waiting for transfers between devices: none -> 157 us  [the longest x8 156 us: collect(): lax.ppermute(going_up, axis, [(d, (d + 1) % ways) for d in range(ways)])]
    all_gather x1, waiting for transfers between devices: 84.5 us -> 0.01 us  [on_device(): lax.all_gather(gate_weight, ('dp', 'ctx'), axis=0, tiled=True)]
    ppermute x0 -> x15, starting transfers between devices: none -> 70.4 us  [the longest x7 55.4 us: collect(): lax.ppermute(going_down, axis, [(d, (d - 1) % ways) for d in range(ways)])]
    psum x3, waiting for transfers between devices: 270 us -> 205 us  [tensor_sum(): return lax.psum(values.astype(jnp.bfloat16), 'tp').astype(jnp.float32)]
    all_gather x1, waiting for transfers between devices: 76.2 us -> 46.6 us  [on_device(): lax.all_gather(up_weight, ('dp', 'ctx'), axis=0, tiled=True)]
  transfers between devices with their start and end apart: 19 -> 34, of which waited for: 16 -> 23; matrix products, arithmetic and copies ran while one was open for 12% -> 14% of each run, Pallas kernels for 0% -> 0%
where the time goes in v1:
time: 2280 us; the launch traced here: 2270 us
  waiting for transfers between devices  1450 us (64%)
  matrix products  401 us (18%)
  blocking collectives  126 us (6%)
  local copies, waits for them, and re-layouts  110 us (5%)
  starting transfers between devices  71.7 us (3%)
  other arithmetic  52.5 us (2%)
  loops' own time  46.6 us (2%)
    reduce_scatter x1, waiting for transfers between devices, on_device(): lax.psum_scatter(grad_down, ('dp', 'ctx'), scatter_dimension=1, tiled=True)  215 us
    reduce_scatter x1, waiting for transfers between devices, on_device(): lax.psum_scatter(grad_up_weight, ('dp', 'ctx'), scatter_dimension=0, tile...  215 us
    reduce_scatter x1, waiting for transfers between devices, on_device(): lax.psum_scatter(grad_gate_weight, ('dp', 'ctx'), scatter_dimension=0, ti...  215 us
    psum x3, waiting for transfers between devices, tensor_sum(): return lax.psum(values.astype(jnp.bfloat16), 'tp').astype(jnp.float32)  205 us
    dot_general x37, matrix products, contract_last(): lax.dot_general(left_rows, right_rows, (((1,), (1,)), ((), ())), preferre...  166 us
    ppermute x8, waiting for transfers between devices, collect(): lax.ppermute(going_up, axis, [(d, (d + 1) % ways) for d in range(ways)])  156 us
    dot_general x27, matrix products, contract_first(): lax.dot_general(left_rows, right_rows, (((0,), (0,)), ((), ())), preferre...  114 us
    unnamed x21, waiting for transfers between devices  103 us
  transfers between devices with their start and end apart: 34, of which 23 were waited for; matrix products, arithmetic and copies ran while one was open for 14% of the time, Pallas kernels for 0%

profile of v1, /device:TPU:0, one launch (start us, length us, event | category | flops | bytes accessed | tf_op | source)
XLA Modules:
  0.0 2273.6 jit_solution(1551617717853152149)
XLA Ops:
  17.5 33.1 %all-gather.10.cloned.1.call-done = bf16[2048,320]{0,1:T(8,128)(2,1)} async-done(((bf16[128,320]{0,1:T(8,128)(2,1)}), bf16[2048,320]{0,1:T(8,128)(2,1)}) %all-gather.10.cloned.1.call-update) | async-done | bytes 1310736 | tf_op jit(solution)/shard_map/all_gather | solution.py:128
  55.7 34.2 %all-gather.12.cloned.1.call-done = bf16[2048,320]{0,1:T(8,128)(2,1)} async-done(((bf16[128,320]{0,1:T(8,128)(2,1)}), bf16[2048,320]{0,1:T(8,128)(2,1)}) %all-gather.12.cloned.1.call-update) | async-done | bytes 1310736 | tf_op jit(solution)/shard_map/all_gather | solution.py:129
  94.0 30.3 %all_gather.35 = bf16[1024,320]{0,1:T(8,128)(2,1)S(1)} all-gather(bf16[128,320]{0,1:T(8,128)(2,1)S(1)} %slice.74), channel_id=1, replica_groups=mesh['dp'=2,'ctx'=8,'tp'=2] {'ctx'}, dimensions={0}, use_global_device_ids=true | all-gather | bytes 737280 | tf_op jit(solution)/shard_map/all_gather | solution.py:142
  127.6 29.9 %all_gather.37 = bf16[1024,320]{0,1:T(8,128)(2,1)S(1)} all-gather(bf16[128,320]{0,1:T(8,128)(2,1)S(1)} %slice.76), channel_id=1, replica_groups=mesh['dp'=2,'ctx'=8,'tp'=2] {'ctx'}, dimensions={0}, use_global_device_ids=true | all-gather | bytes 737280 | tf_op jit(solution)/shard_map/all_gather | solution.py:143
  170.9 124.1 %while.34 = (s32[]{:T(128)}, bf16[10,640,64]{1,2,0:T(8,128)(2,1)}, f32[10,640]{1,0:T(8,128)}, s32[10]{0:T(128)S(1)}, bf16[640,640]{1,0:T(8,128)(2,1)S(1)}, /*ind...) while((s32[]{:T(128)}, bf16[10,640,64]{1,2,0:T(8,128)(2,1)}, ...), condition=%wide.region_6.7_spmd.clone.clone, body=%wide.region_3.6_spmd.clone.sunk.clone | while | flops 263454112 | bytes 28690356 | solution.py:169
  365.0 17.1 collective-permute-done.4
  396.1 23.0 %collective-permute-done.6 = bf16[128,2560]{1,0:T(8,128)(2,1)S(1)} collective-permute-done((bf16[128,2560]{1,0:T(8,128)(2,1)S(1)}, bf16[128,2560]{1,0:T(8,128)(2,1)S(1)}, u32[]{:S(2)}, u32[]{:S(2)}) %collective-permute-start.6) | collective-permute-done | bytes 655392 | tf_op jit(solution)/shard_map/ppermute | solution.py:16
  428.1 35.6 %collective-permute-done.8 = bf16[128,2560]{1,0:T(8,128)(2,1)S(1)} collective-permute-done((bf16[128,2560]{1,0:T(8,128)(2,1)S(1)}, bf16[128,2560]{1,0:T(8,128)(2,1)S(1)}, u32[]{:S(2)}, u32[]{:S(2)}) %collective-permute-start.8) | collective-permute-done | bytes 655392 | tf_op jit(solution)/shard_map/ppermute | solution.py:16
  478.0 27.6 %collective-permute-done.10 = bf16[128,2560]{1,0:T(8,128)(2,1)S(1)} collective-permute-done((bf16[128,2560]{1,0:T(8,128)(2,1)S(1)}, bf16[128,2560]{1,0:T(8,128)(2,1)S(1)}, u32[]{:S(2)}, u32[]{:S(2)}) %collective-permute-start.10) | collective-permute-done | bytes 655392 | tf_op jit(solution)/shard_map/ppermute | solution.py:16
  520.0 17.0 collective-permute-done.12
  574.7 64.3 %all-gather.18.cloned.1.call-done = bf16[2560,2048]{1,0:T(8,128)(2,1)} async-done(((bf16[2560,128]{1,0:T(8,128)(2,1)}), bf16[2560,2048]{1,0:T(8,128)(2,1)}) %all-gather.18.cloned.1.call-update) | async-done | bytes 10485776 | tf_op jit(solution)/shard_map/all_gather | solution.py:177
  681.0 46.6 %all-gather.20.cloned.1.call-done = bf16[2048,2560]{1,0:T(8,128)(2,1)} async-done(((bf16[128,2560]{1,0:T(8,128)(2,1)}), bf16[2048,2560]{1,0:T(8,128)(2,1)}) %all-gather.20.cloned.1.call-update) | async-done | bytes 10485776 | tf_op jit(solution)/shard_map/all_gather | solution.py:210
  740.6 72.6 %all-reduce.12.cloned.1.call-done = bf16[640,2048]{1,0:T(8,128)(2,1)} async-done(((bf16[640,2048]{1,0:T(8,128)(2,1)}), bf16[640,2048]{1,0:T(8,128)(2,1)}) %all-reduce.12.cloned.1.call-update) | async-done | bytes 2621456 | tf_op jit(solution)/shard_map/psum | solution.py:72
  827.9 208.5 %while.35 = (s32[]{:T(128)}, f32[1536,320]{0,1:T(8,128)}, f32[1536,320]{0,1:T(8,128)}, f32[10,640,64]{1,2,0:T(8,128)}, s32[10]{0:T(128)S(1)}, /*index=5*/s32[]{:...) while((s32[]{:T(128)}, f32[1536,320]{0,1:T(8,128)}, ...), condition=%wide.region_14.15_spmd.clone.clone, body=%wide.region_12.14_spmd.clone.sunk.clone | while | flops 643104128 | bytes 48826372 | solution.py:246
  1067.9 34.9 %reduce-scatter.30.cloned.1.call-done = bf16[128,320]{1,0:T(8,128)(2,1)} async-done(((bf16[1024,320]{1,0:T(8,128)(2,1)}), bf16[128,320]{1,0:T(8,128)(2,1)}) %reduce-scatter.30.cloned.1.call-update) | async-done | bytes 81936
  1104.7 63.8 %reduce-scatter.28.cloned.1.call-done = bf16[128,320]{1,0:T(8,128)(2,1)} async-done(((bf16[1024,320]{1,0:T(8,128)(2,1)}), bf16[128,320]{1,0:T(8,128)(2,1)}) %reduce-scatter.28.cloned.1.call-update) | async-done | bytes 81936
  1187.7 132.1 %all-reduce.14.cloned.1.call-done = (bf16[640,2048]{1,0:T(8,128)(2,1)}, bf16[640,5,64]{0,2,1:T(8,128)(2,1)}, bf16[640,2048]{1,0:T(8,128)(2,1)}, bf16[640,320]{0,1:T(8,128)(2,1)}) async-done(((bf16[640,2048]{1,0:T(8,128)(2,1)}, bf16[640,5,64]{0,2,1:T(8,128)(2,1)}, bf16[640,2048]{1,0:T(8,128)(2,1)}, bf16[640,320]{0,1:T(8,128)(2,1)}), (bf16[640,2048]{1,0:T(8,128)(2,1)}, bf16[640,5,64]{0,2,1:T(8,128)(2,1)}, ...) | async-done | bytes 6062096 | tf_op jit(solution)/shard_map/psum | solution.py:72
  1399.2 60.7 %all-reduce.4 = (f32[2048]{0:T(1024)}, f32[64]{0:T(128)}, f32[64]{0:T(128)}, f32[2048]{0:T(1024)}) all-reduce(f32[2048]{0:T(1024)S(1)} %get-tuple-element.423, bf16[64]{0:T(256)(128)(2,1)S(1)} %psum.84, f32[64]{0:T(128)S(1)} %get-tuple-element.427, f32[2048]{0:T(1024)S(1)} %copy-done.49), channel_id=1, replica_groups=mesh['dp'=2,'ctx'=8,'tp'=2] {'dp','ctx'}, use_global_device_ids=true, to_apply=%region_24.25 | all-reduce | flops 4224 | bytes 33664 | tf_op jit(solution)/shard_map/psum | solution.py:294
  1459.9 26.3 %reduce-scatter.14.cloned.1.call-done = f32[128,640]{1,0:T(8,128)} async-done(((f32[2048,640]{1,0:T(8,128)}), f32[128,640]{1,0:T(8,128)}) %reduce-scatter.14.cloned.1.call-update) | async-done | bytes 327696 | tf_op jit(solution)/shard_map/reduce_scatter | solution.py:284
  1486.2 67.5 %reduce-scatter.16.cloned.1.call-done = f32[128,320]{0,1:T(8,128)} async-done(((f32[2048,320]{0,1:T(8,128)}), f32[128,320]{0,1:T(8,128)}) %reduce-scatter.16.cloned.1.call-update) | async-done | bytes 163856 | tf_op jit(solution)/shard_map/reduce_scatter | solution.py:285
  1553.7 67.6 %reduce-scatter.18.cloned.1.call-done = f32[128,320]{0,1:T(8,128)} async-done(((f32[2048,320]{0,1:T(8,128)}), f32[128,320]{0,1:T(8,128)}) %reduce-scatter.18.cloned.1.call-update) | async-done | bytes 163856 | tf_op jit(solution)/shard_map/reduce_scatter | solution.py:286
  1621.3 214.9 %reduce-scatter.22.cloned.1.call-done = f32[128,2560]{1,0:T(8,128)} async-done(((f32[2048,2560]{1,0:T(8,128)}), f32[128,2560]{1,0:T(8,128)}) %reduce-scatter.22.cloned.1.call-update) | async-done | bytes 1310736 | tf_op jit(solution)/shard_map/reduce_scatter | solution.py:287
  1836.3 215.1 %reduce-scatter.24.cloned.1.call-done = f32[128,2560]{1,0:T(8,128)} async-done(((f32[2048,2560]{1,0:T(8,128)}), f32[128,2560]{1,0:T(8,128)}) %reduce-scatter.24.cloned.1.call-update) | async-done | bytes 1310736 | tf_op jit(solution)/shard_map/reduce_scatter | solution.py:288
  2051.3 215.3 %reduce-scatter.26.cloned.1.call-done = f32[2560,128]{1,0:T(8,128)} async-done(((f32[2560,2048]{1,0:T(8,128)}), f32[2560,128]{1,0:T(8,128)}) %reduce-scatter.26.cloned.1.call-update) | async-done | bytes 1310736 | tf_op jit(solution)/shard_map/reduce_scatter | solution.py:292
  (501 shorter events, 681.4 us)
Async XLA Ops:
  7.2 43.4 %all-gather.10.cloned.1.call-start = ((), (), s32[]{:S(2)}) async-start(), calls=%async_computation.10 | async-start | bytes 1392640 | tf_op jit(solution)/shard_map/all_gather | solution.py:128
  8.0 81.9 %all-gather.12.cloned.1.call-start = ((), (), s32[]{:S(2)}) async-start(), calls=%async_computation.11 | async-start | bytes 1392640 | tf_op jit(solution)/shard_map/all_gather | solution.py:129
  8.7 153.1 %all-gather.8.cloned.1.call-start = ((), (), s32[]{:S(2)}) async-start(), calls=%async_computation.9 | async-start | bytes 2785280 | tf_op jit(solution)/shard_map/all_gather | solution.py:127
  9.5 285.6 %all-gather.14.cloned.1.call-start = ((), (), s32[]{:S(2)}) async-start(), calls=%async_computation.12 | async-start | bytes 2785280 | tf_op jit(solution)/shard_map/all_gather | solution.py:176
  10.0 546.7 %all-reduce.10.cloned.1.call-start = ((), (), s32[]{:S(2)}) async-start(), calls=%async_computation.13 | async-start | bytes 5242880 | tf_op jit(solution)/shard_map/psum | solution.py:72
  300.9 261.7 %all-gather.16.cloned.1.call-start = ((), (), s32[]{:S(2)}) async-start(), calls=%async_computation.14 | async-start | bytes 11141120 | tf_op jit(solution)/shard_map/all_gather | solution.py:187
  301.5 337.6 %all-gather.18.cloned.1.call-start = ((), (), s32[]{:S(2)}) async-start(), calls=%async_computation.15 | async-start | bytes 11141120 | tf_op jit(solution)/shard_map/all_gather | solution.py:177
  302.2 425.4 %all-gather.20.cloned.1.call-start = ((), (), s32[]{:S(2)}) async-start(), calls=%async_computation.16 | async-start | bytes 11141120 | tf_op jit(solution)/shard_map/all_gather | solution.py:210
  303.0 510.3 %all-reduce.12.cloned.1.call-start = ((), (), s32[]{:S(2)}) async-start(), calls=%async_computation.17 | async-start | bytes 5242880 | tf_op jit(solution)/shard_map/psum | solution.py:72
  382.2 36.9 %collective-permute-start.6 = (bf16[128,2560]{1,0:T(8,128)(2,1)S(1)}, bf16[128,2560]{1,0:T(8,128)(2,1)S(1)}, u32[]{:S(2)}, u32[]{:S(2)}) collective-permute-start(bf16[128,2560]{1,0:T(8,128)(2,1)S(1)} %collective-permute-done.4), channel_id=1, source_target_pairs={{0,2},{2,4},{4,6},{6,8},{8,10},{10,12},{12,14},{14,16},{16,18},{18... | collective-permute-start | bytes 1966088 | tf_op jit(solution)/shard_map/ppermute | solution.py:16
  419.1 44.6 %collective-permute-start.8 = (bf16[128,2560]{1,0:T(8,128)(2,1)S(1)}, bf16[128,2560]{1,0:T(8,128)(2,1)S(1)}, u32[]{:S(2)}, u32[]{:S(2)}) collective-permute-start(bf16[128,2560]{1,0:T(8,128)(2,1)S(1)} %collective-permute-done.6), channel_id=1, source_target_pairs={{0,2},{2,4},{4,6},{6,8},{8,10},{10,12},{12,14},{14,16},{16,18},{18... | collective-permute-start | bytes 1966088 | tf_op jit(solution)/shard_map/ppermute | solution.py:16
  421.6 44.6 %collective-permute-start.9 = (bf16[128,2560]{1,0:T(8,128)(2,1)S(1)}, bf16[128,2560]{1,0:T(8,128)(2,1)S(1)}, u32[]{:S(2)}, u32[]{:S(2)}) collective-permute-start(bf16[128,2560]{1,0:T(8,128)(2,1)S(1)} %collective-permute-done.7), channel_id=1, source_target_pairs={{0,30},{2,0},{4,2},{6,4},{8,6},{10,8},{12,10},{14,12},{16,14},{18,... | collective-permute-start | bytes 1966088 | tf_op jit(solution)/shard_map/ppermute | solution.py:19
  463.6 42.0 %collective-permute-start.10 = (bf16[128,2560]{1,0:T(8,128)(2,1)S(1)}, bf16[128,2560]{1,0:T(8,128)(2,1)S(1)}, u32[]{:S(2)}, u32[]{:S(2)}) collective-permute-start(bf16[128,2560]{1,0:T(8,128)(2,1)S(1)} %collective-permute-done.8), channel_id=1, source_target_pairs={{0,2},{2,4},{4,6},{6,8},{8,10},{10,12},{12,14},{14,16},{16,18},{18... | collective-permute-start | bytes 1966088 | tf_op jit(solution)/shard_map/ppermute | solution.py:16
  466.1 42.0 %collective-permute-start.11 = (bf16[128,2560]{1,0:T(8,128)(2,1)S(1)}, bf16[128,2560]{1,0:T(8,128)(2,1)S(1)}, u32[]{:S(2)}, u32[]{:S(2)}) collective-permute-start(bf16[128,2560]{1,0:T(8,128)(2,1)S(1)} %collective-permute-done.9), channel_id=1, source_target_pairs={{0,30},{2,0},{4,2},{6,4},{8,6},{10,8},{12,10},{14,12},{16,14},{18,... | collective-permute-start | bytes 1966088 | tf_op jit(solution)/shard_map/ppermute | solution.py:19
  740.6 362.3 %reduce-scatter.30.cloned.1.call-start = ((), (), s32[]{:S(2)}) async-start(), calls=%async_computation.26 | async-start | bytes 884736
  1040.3 128.2 %reduce-scatter.28.cloned.1.call-start = ((), (), s32[]{:S(2)}) async-start(), calls=%async_computation.25 | async-start | bytes 884736
  1058.8 261.0 %all-reduce.14.cloned.1.call-start = ((), (), s32[]{:S(2)}) async-start(), calls=%async_computation.27 | async-start | bytes 12124160 | tf_op jit(solution)/shard_map/psum | solution.py:72
  1170.4 289.6 %reduce-scatter.20.cloned.1.call-start = ((), (), s32[]{:S(2)}) async-start(), calls=%async_computation.21 | async-start | bytes 5570560 | tf_op jit(solution)/shard_map/reduce_scatter | solution.py:291
  1179.7 306.5 %reduce-scatter.14.cloned.1.call-start = ((), (), s32[]{:S(2)}) async-start(), calls=%async_computation.18 | async-start | bytes 5570560 | tf_op jit(solution)/shard_map/reduce_scatter | solution.py:284
  1187.4 366.3 %reduce-scatter.16.cloned.1.call-start = ((), (), s32[]{:S(2)}) async-start(), calls=%async_computation.19 | async-start | bytes 2785280 | tf_op jit(solution)/shard_map/reduce_scatter | solution.py:285
  1326.4 294.9 %reduce-scatter.18.cloned.1.call-start = ((), (), s32[]{:S(2)}) async-start(), calls=%async_computation.20 | async-start | bytes 2785280 | tf_op jit(solution)/shard_map/reduce_scatter | solution.py:286
  1330.9 505.3 %reduce-scatter.22.cloned.1.call-start = ((), (), s32[]{:S(2)}) async-start(), calls=%async_computation.22 | async-start | bytes 22282240 | tf_op jit(solution)/shard_map/reduce_scatter | solution.py:287
  1346.2 705.1 %reduce-scatter.24.cloned.1.call-start = ((), (), s32[]{:S(2)}) async-start(), calls=%async_computation.23 | async-start | bytes 22282240 | tf_op jit(solution)/shard_map/reduce_scatter | solution.py:288
  1361.2 905.5 %reduce-scatter.26.cloned.1.call-start = ((), (), s32[]{:S(2)}) async-start(), calls=%async_computation.24 | async-start | bytes 22282240 | tf_op jit(solution)/shard_map/reduce_scatter | solution.py:292
  (92 other events, 1845.7 us)
Sparse Core Ops, SparseCore 0:
  10.1 40.4 all-gather.9
  52.7 37.0 all-gather.11
  92.1 45.5 all-gather.7
  139.6 45.6 all-gather.13
  301.0 72.1 all-reduce.9
  375.5 155.8 all-gather.15
  533.7 105.3 all-gather.17
  641.5 86.0 all-gather.19
  740.7 72.4 all-reduce.11
  1040.4 62.4 reduce-scatter.29
  1107.1 61.3 reduce-scatter.27
  1171.6 148.2 all-reduce.13
  1324.8 78.4 reduce-scatter.19
  1408.0 78.1 reduce-scatter.13
  1490.9 62.8 reduce-scatter.15
  1558.4 62.8 reduce-scatter.17
  1626.4 209.8 reduce-scatter.21
  1841.3 209.9 reduce-scatter.23
  2056.6 209.9 reduce-scatter.25
